TPU v7x, 32 devices: a whole 2x2x4 slice. The times are simulated.
32 devices in a mesh: dp: 8 (over z, x), tensor: 4 (over y, core).
Axes of the slice: x: 2, y: 2, z: 4, core: 2. Of those that a mesh axis runs over, the one named last changes fastest.
Arguments:
- gradients: bfloat16 [8, 4096, 4096], P('dp', None, 'tensor'), may hold values from -300 to 300
- feedback: bfloat16 [8, 4096, 4096], P('dp', None, 'tensor'), may hold values from -12 to 12
- warm_start: float32 [4096, 64], P('tensor'), may hold values from -0.09375 to 0.09375
Outputs:
- projected: float32 [4096, 64], P('tensor')
- refreshed: float32 [4096, 64], P('tensor')
- decompressed: bfloat16 [4096, 4096], P(None, 'tensor')
All inputs are finite; a program needn't handle non-finite values.
Results may differ from a plain program's by a relative error of at most 0.001.
Values sent between devices are 32-bit elements; how exact they have to be, the bound alone decides.
A program may use at most 128 MiB of HBM per device.

v0:
```python
import jax
import jax.numpy as jnp
from jax import lax
from jax.sharding import PartitionSpec as P

HIGHEST = lax.Precision.HIGHEST


def on_device(gradients, feedback, warm_start):
    corrected = gradients[0].astype(jnp.float32) + feedback[0].astype(jnp.float32)
    members = lax.axis_size("dp")
    partial_value = lax.psum_scatter(
        jnp.dot(corrected, warm_start, precision=HIGHEST), "tensor", scatter_dimension=0, tiled=True
    )
    projected = lax.psum(partial_value, "dp") / members
    gram_matrix = lax.psum(jnp.dot(projected.T, projected, precision=HIGHEST), "tensor")
    factor = jnp.linalg.cholesky(gram_matrix)
    orth_shard = lax.linalg.triangular_solve(
        factor, projected, left_side=False, lower=True, transpose_a=True
    )
    basis = lax.all_gather(orth_shard, "tensor", axis=0, tiled=True)
    local_right = lax.dot_general(corrected, basis, (((0,), (0,)), ((), ())), precision=HIGHEST)
    refreshed = lax.psum(local_right, "dp") / members
    decompressed = jnp.dot(basis, refreshed.T, precision=HIGHEST).astype(jnp.bfloat16)
    return (projected, refreshed, decompressed)


def solution(mesh):
    return jax.shard_map(
        on_device,
        mesh=mesh,
        in_specs=(P("dp", None, "tensor"), P("dp", None, "tensor"), P("tensor", None)),
        out_specs=(P("tensor", None), P("tensor", None), P(None, "tensor")),
        check_vma=False,
    )
```

profile of v0, /device:TPU:0, one launch (start us, length us, event | category | flops | bytes accessed | tf_op | source)
XLA Modules:
  0.0 286.7 jit_solution(11949851245497997149)
XLA Ops:
  7.2 0.0 copy-start
  7.2 0.0 reduce-scatter.2.cloned.1.call-start
  7.2 0.9 copy-done
  8.1 22.3 %fusion.2 = f32[4096,64]{0,1:T(8,128)} fusion(f32[1024,64]{0,1:T(8,128)S(1)} %copy-done, bf16[1,4096,1024]{2,1,0:T(8,128)(2,1)} %param.4, bf16[1,4096,1024]{2,1,0:T(8,128)(2,1)} %param.3), kind=kOutput, calls=%fused_computation.2 | convolution fusion | flops 3233808384 | bytes 18087936 | tf_op jit(solution)/shard_map/dot_general | solution.py:13
  30.4 0.0 reduce-scatter.2.cloned.1.call-update
  30.5 0.0 all-reduce.3.cloned.1.call-start
  30.5 27.6 %reduce-scatter.2.cloned.1.call-done = f32[1024,64]{0,1:T(8,128)} async-done(((f32[4096,64]{0,1:T(8,128)}), f32[1024,64]{0,1:T(8,128)}) %reduce-scatter.2.cloned.1.call-update) | async-done | bytes 262160 | tf_op jit(solution)/shard_map/reduce_scatter | solution.py:12
  58.1 0.0 all-reduce.3.cloned.1.call-update
  58.1 0.0 all-gather.2.cloned.1.call-start
  58.2 74.3 %all-reduce.3.cloned.1.call-done = f32[1024,64]{0,1:T(8,128)} async-done(((f32[1024,64]{0,1:T(8,128)}), f32[1024,64]{0,1:T(8,128)}) %all-reduce.3.cloned.1.call-update) | async-done | bytes 262160 | tf_op jit(solution)/shard_map/psum | solution.py:15
  132.5 1.0 broadcast_multiply_fusion.1
  133.5 0.0 copy-start.2
  133.5 0.4 fusion.8
  133.9 10.3 %psum.22 = f32[64,64]{0,1:T(8,128)S(1)} all-reduce(f32[64,64]{0,1:T(8,128)S(1)} %fusion.8), channel_id=1, replica_groups=mesh['dp'=8,'tensor'=4] {'tensor'}, use_global_device_ids=true, to_apply=%region_2.0 | all-reduce | flops 4096 | bytes 32768 | tf_op jit(solution)/shard_map/psum | solution.py:16
  144.2 0.1 copy.7
  144.2 5.8 %cholesky.16 = f32[64,64]{1,0:T(8,128)S(1)} custom-call(f32[64,64]{1,0:T(8,128)S(1)} %fusion.7), custom_call_target="Cholesky" | custom-call | tf_op jit(solution)/shard_map/jit(cholesky)/cholesky | solution.py:17
  150.1 0.6 compare_reduce_fusion
  150.8 0.7 fusion.4
  151.4 4.9 %custom-call.6 = f32[1,64,64]{1,2,0:T(8,128)S(1)} custom-call(f32[1,64,64]{2,1,0:T(8,128)S(1)} %fusion.4), custom_call_target="InvertDiagBlocksLowerTriangular" | custom-call | tf_op jit(solution)/shard_map/triangular_solve | solution.py:18
  156.3 1.1 fusion.5
  157.5 0.0 all-gather.2.cloned.1.call-update
  157.5 0.2 all-reduce.5.cloned.1.call-start
  157.7 16.0 %all-gather.2.cloned.1.call-done = f32[4096,64]{0,1:T(8,128)} async-done(((f32[1024,64]{0,1:T(8,128)}), f32[4096,64]{0,1:T(8,128)}) %all-gather.2.cloned.1.call-update) | async-done | bytes 1048592 | tf_op jit(solution)/shard_map/all_gather | solution.py:21
  173.7 0.0 copy-start.1
  173.7 19.0 %fusion = f32[1024,64]{0,1:T(8,128)} fusion(f32[4096,64]{0,1:T(8,128)} %all-gather.2.cloned.1.call-done, bf16[1,4096,1024]{2,1,0:T(8,128)(2,1)} %param.4, bf16[1,4096,1024]{2,1,0:T(8,128)(2,1)} %param.3), kind=kOutput, calls=%fused_computation | convolution fusion | flops 3233808384 | bytes 18087936 | tf_op jit(solution)/shard_map/dot_general | solution.py:22
  192.7 0.0 copy-done.2
  192.7 0.0 all-reduce.5.cloned.1.call-update
  192.8 71.2 %all-reduce.5.cloned.1.call-done = f32[1024,64]{0,1:T(8,128)} async-done(((f32[1024,64]{0,1:T(8,128)}), f32[1024,64]{0,1:T(8,128)}) %all-reduce.5.cloned.1.call-update) | async-done | bytes 262160 | tf_op jit(solution)/shard_map/psum | solution.py:23
  263.9 1.0 broadcast_multiply_fusion
  264.9 0.0 copy-done.1
  264.9 0.0 copy-start.3
  264.9 15.3 %convolution_convert_fusion = bf16[4096,1024]{1,0:T(8,128)(2,1)} fusion(f32[4096,64]{0,1:T(8,128)S(1)} %copy-done.1, f32[1024,64]{0,1:T(8,128)S(1)} %broadcast_multiply_fusion), kind=kOutput, calls=%fused_computation.5 | convolution fusion | flops 3225419776 | bytes 9699328 | tf_op jit(solution)/shard_map/dot_general | solution.py:24
  280.2 0.0 copy-done.3
  (2 shorter events, 0.0 us)
Async XLA Ops:
  7.2 1.0 copy-start
  7.2 50.9 %reduce-scatter.2.cloned.1.call-start = ((), (), s32[]{:S(2)}) async-start(), calls=%async_computation.1 | async-start | bytes 1310720 | tf_op jit(solution)/shard_map/reduce_scatter | solution.py:12
  30.5 102.1 %all-reduce.3.cloned.1.call-start = ((), (), s32[]{:S(2)}) async-start(), calls=%async_computation.2 | async-start | bytes 524288 | tf_op jit(solution)/shard_map/psum | solution.py:15
  58.1 115.6 %all-gather.2.cloned.1.call-start = ((), (), s32[]{:S(2)}) async-start(), calls=%async_computation.3 | async-start | bytes 1310720 | tf_op jit(solution)/shard_map/all_gather | solution.py:21
  133.5 59.2 %copy-start.2 = (f32[1024,64]{0,1:T(8,128)}, f32[1024,64]{0,1:T(8,128)S(1)}, u32[]{:S(2)}) copy-start(f32[1024,64]{0,1:T(8,128)S(1)} %broadcast_multiply_fusion.1) | copy-start | bytes 786436
  157.5 106.4 %all-reduce.5.cloned.1.call-start = ((), (), s32[]{:S(2)}) async-start(), calls=%async_computation.4 | async-start | bytes 524288 | tf_op jit(solution)/shard_map/psum | solution.py:23
  173.7 91.2 %copy-start.1 = (f32[4096,64]{0,1:T(8,128)S(1)}, f32[4096,64]{0,1:T(8,128)}, u32[]{:S(2)}) copy-start(f32[4096,64]{0,1:T(8,128)} %all-gather.2.cloned.1.call-done) | copy-start | bytes 3145732
  264.9 15.3 %copy-start.3 = (f32[1024,64]{0,1:T(8,128)}, f32[1024,64]{0,1:T(8,128)S(1)}, u32[]{:S(2)}) copy-start(f32[1024,64]{0,1:T(8,128)S(1)} %broadcast_multiply_fusion) | copy-start | bytes 786436
Sparse Core Ops, SparseCore 0:
  30.6 27.4 reduce-scatter.1
  61.5 71.0 all-reduce.2
  157.6 16.0 all-gather.1
  192.9 71.0 all-reduce.4
where the time goes:
time: 287 us
  waiting for transfers between devices  189 us (66%)
  matrix products  58.1 us (20%)
  other arithmetic  14 us (5%)
  between operations  13.8 us (5%)
  blocking collectives  10.3 us (4%)
    psum x1, waiting for transfers between devices, on_device(): projected = lax.psum(partial_value, 'dp') / members  74.3 us
    psum x1, waiting for transfers between devices, on_device(): refreshed = lax.psum(local_right, 'dp') / members  71.2 us
    reduce_scatter x1, waiting for transfers between devices, on_device(): lax.psum_scatter(jnp.dot(corrected, warm_start, precision=HIGHEST), 'tens...  27.6 us
    dot_general x1, matrix products, on_device(): jnp.dot(corrected, warm_start, precision=HIGHEST)  22.3 us
    dot_general x1, matrix products, on_device(): lax.dot_general(corrected, basis, (((0,), (0,)), ((), ())), precision=HIG...  19 us
    all_gather x1, waiting for transfers between devices, on_device(): basis = lax.all_gather(orth_shard, 'tensor', axis=0, tiled=True)  16 us
    dot_general x1, matrix products, on_device(): jnp.dot(basis, refreshed.T, precision=HIGHEST).astype(jnp.bfloat16)  15.3 us
    psum x1, blocking collectives, on_device(): lax.psum(jnp.dot(projected.T, projected, precision=HIGHEST), 'tensor')  10.3 us
  transfers between devices with their start and end apart: 4, of which 4 were waited for; matrix products, arithmetic and copies ran while one was open for 0% of the time, Pallas kernels for 0%

commit v1 on v0

--- a/solution.py
+++ b/solution.py
@@ -20,7 +20,7 @@
     )
     basis = lax.all_gather(orth_shard, "tensor", axis=0, tiled=True)
     local_right = lax.dot_general(corrected, basis, (((0,), (0,)), ((), ())), precision=HIGHEST)
-    refreshed = lax.psum(local_right, "dp") / members
+    refreshed = jax.lax.all_gather(local_right, axis_name="dp").sum(axis=0) / members
     decompressed = jnp.dot(basis, refreshed.T, precision=HIGHEST).astype(jnp.bfloat16)
     return (projected, refreshed, decompressed)
 

time: 287 us -> 267 us (0.930)
  waiting for transfers between devices: 189 us -> 167 us
    psum x1 -> x0, waiting for transfers between devices: 71.2 us -> none  [on_device(): refreshed = lax.psum(local_right, 'dp') / members]
    all_gather x0 -> x1, waiting for transfers between devices: none -> 49.2 us  [on_device(): jax.lax.all_gather(local_right, axis_name='dp').sum(axis=0) / members]
where the time goes in v1:
time: 267 us
  waiting for transfers between devices  167 us (63%)
  matrix products  58.1 us (22%)
  between operations  13.9 us (5%)
  other arithmetic  13.6 us (5%)
  blocking collectives  10.3 us (4%)
  local copies, waits for them, and re-layouts  3.78 us (1%)
    psum x1, waiting for transfers between devices, on_device(): projected = lax.psum(partial_value, 'dp') / members  74.3 us
    all_gather x1, waiting for transfers between devices, on_device(): jax.lax.all_gather(local_right, axis_name='dp').sum(axis=0) / members  49.2 us
    reduce_scatter x1, waiting for transfers between devices, on_device(): lax.psum_scatter(jnp.dot(corrected, warm_start, precision=HIGHEST), 'tens...  27.6 us
    dot_general x1, matrix products, on_device(): jnp.dot(corrected, warm_start, precision=HIGHEST)  22.3 us
    dot_general x1, matrix products, on_device(): lax.dot_general(corrected, basis, (((0,), (0,)), ((), ())), precision=HIG...  19 us
    all_gather x1, waiting for transfers between devices, on_device(): basis = lax.all_gather(orth_shard, 'tensor', axis=0, tiled=True)  16 us
    dot_general x1, matrix products, on_device(): jnp.dot(basis, refreshed.T, precision=HIGHEST).astype(jnp.bfloat16)  15.3 us
    psum x1, blocking collectives, on_device(): lax.psum(jnp.dot(projected.T, projected, precision=HIGHEST), 'tensor')  10.3 us
  transfers between devices with their start and end apart: 4, of which 4 were waited for; matrix products, arithmetic and copies ran while one was open for 0% of the time, Pallas kernels for 0%

profile of v1, /device:TPU:0, one launch (start us, length us, event | category | flops | bytes accessed | tf_op | source)
XLA Modules:
  0.0 267.1 jit_solution(6046427685905476115)
XLA Ops:
  7.2 0.0 copy-start
  7.2 0.0 reduce-scatter.2.cloned.1.call-start
  7.2 0.9 copy-done
  8.1 22.3 %fusion.2 = f32[4096,64]{0,1:T(8,128)} fusion(f32[1024,64]{0,1:T(8,128)S(1)} %copy-done, bf16[1,4096,1024]{2,1,0:T(8,128)(2,1)} %param.4, bf16[1,4096,1024]{2,1,0:T(8,128)(2,1)} %param.3), kind=kOutput, calls=%fused_computation.2 | convolution fusion | flops 3233808384 | bytes 18087936 | tf_op jit(solution)/shard_map/dot_general | solution.py:13
  30.4 0.0 reduce-scatter.2.cloned.1.call-update
  30.5 0.0 all-reduce.2.cloned.1.call-start
  30.5 27.6 %reduce-scatter.2.cloned.1.call-done = f32[1024,64]{0,1:T(8,128)} async-done(((f32[4096,64]{0,1:T(8,128)}), f32[1024,64]{0,1:T(8,128)}) %reduce-scatter.2.cloned.1.call-update) | async-done | bytes 262160 | tf_op jit(solution)/shard_map/reduce_scatter | solution.py:12
  58.1 0.0 all-reduce.2.cloned.1.call-update
  58.1 0.0 all-gather.4.cloned.1.call-start
  58.2 74.3 %all-reduce.2.cloned.1.call-done = f32[1024,64]{0,1:T(8,128)} async-done(((f32[1024,64]{0,1:T(8,128)}), f32[1024,64]{0,1:T(8,128)}) %all-reduce.2.cloned.1.call-update) | async-done | bytes 262160 | tf_op jit(solution)/shard_map/psum | solution.py:15
  132.5 1.0 broadcast_multiply_fusion.1
  133.5 0.0 copy-start.2
  133.5 0.4 fusion.8
  133.9 10.3 %psum.15 = f32[64,64]{0,1:T(8,128)S(1)} all-reduce(f32[64,64]{0,1:T(8,128)S(1)} %fusion.8), channel_id=1, replica_groups=mesh['dp'=8,'tensor'=4] {'tensor'}, use_global_device_ids=true, to_apply=%region_2.0 | all-reduce | flops 4096 | bytes 32768 | tf_op jit(solution)/shard_map/psum | solution.py:16
  144.2 0.1 copy.7
  144.2 5.8 %cholesky.16 = f32[64,64]{1,0:T(8,128)S(1)} custom-call(f32[64,64]{1,0:T(8,128)S(1)} %fusion.7), custom_call_target="Cholesky" | custom-call | tf_op jit(solution)/shard_map/jit(cholesky)/cholesky | solution.py:17
  150.1 0.6 compare_reduce_fusion
  150.8 0.7 fusion.4
  151.4 4.9 %custom-call.6 = f32[1,64,64]{1,2,0:T(8,128)S(1)} custom-call(f32[1,64,64]{2,1,0:T(8,128)S(1)} %fusion.4), custom_call_target="InvertDiagBlocksLowerTriangular" | custom-call | tf_op jit(solution)/shard_map/triangular_solve | solution.py:18
  156.3 1.1 fusion.5
  157.5 0.0 all-gather.4.cloned.1.call-update
  157.5 0.2 all-gather.6.cloned.1.call-start
  157.7 16.0 %all-gather.4.cloned.1.call-done = f32[4096,64]{0,1:T(8,128)} async-done(((f32[1024,64]{0,1:T(8,128)}), f32[4096,64]{0,1:T(8,128)}) %all-gather.4.cloned.1.call-update) | async-done | bytes 1048592 | tf_op jit(solution)/shard_map/all_gather | solution.py:21
  173.7 0.0 copy-start.1
  173.7 19.0 %fusion = f32[1024,64]{0,1:T(8,128)} fusion(f32[4096,64]{0,1:T(8,128)} %all-gather.4.cloned.1.call-done, bf16[1,4096,1024]{2,1,0:T(8,128)(2,1)} %param.4, bf16[1,4096,1024]{2,1,0:T(8,128)(2,1)} %param.3), kind=kOutput, calls=%fused_computation | convolution fusion | flops 3233808384 | bytes 18087936 | tf_op jit(solution)/shard_map/dot_general | solution.py:22
  192.7 0.0 copy-done.2
  192.7 0.0 all-gather.6.cloned.1.call-update
  192.7 49.2 %all-gather.6.cloned.1.call-done = f32[8192,64]{0,1:T(8,128)} async-done(((f32[1024,64]{0,1:T(8,128)}), f32[8192,64]{0,1:T(8,128)}) %all-gather.6.cloned.1.call-update) | async-done | bytes 2097168 | tf_op jit(solution)/shard_map/all_gather | solution.py:23
  242.0 2.8 %copy.9 = f32[8,8,8,1024]{3,2,1,0:T(8,128)S(1)} copy(f32[8,8,8,1024]{3,1,2,0:T(8,128)} %bitcast.26) | data formatting | bytes 4194304
  244.7 0.5 bitcast_reduce_fusion
  245.3 0.0 copy-done.1
  245.3 0.0 copy-start.3
  245.3 15.3 %convolution_convert_fusion = bf16[4096,1024]{1,0:T(8,128)(2,1)} fusion(f32[4096,64]{0,1:T(8,128)S(1)} %copy-done.1, f32[1024,64]{0,1:T(8,128)S(1)} %broadcast_multiply_fusion), kind=kOutput, calls=%fused_computation.5 | convolution fusion | flops 3225419776 | bytes 9699328 | tf_op jit(solution)/shard_map/dot_general | solution.py:24
  260.6 0.0 copy-done.3
  (3 shorter events, 0.1 us)
Async XLA Ops:
  7.2 1.0 copy-start
  7.2 50.9 %reduce-scatter.2.cloned.1.call-start = ((), (), s32[]{:S(2)}) async-start(), calls=%async_computation.1 | async-start | bytes 1310720 | tf_op jit(solution)/shard_map/reduce_scatter | solution.py:12
  30.5 102.1 %all-reduce.2.cloned.1.call-start = ((), (), s32[]{:S(2)}) async-start(), calls=%async_computation.2 | async-start | bytes 524288 | tf_op jit(solution)/shard_map/psum | solution.py:15
  58.1 115.6 %all-gather.4.cloned.1.call-start = ((), (), s32[]{:S(2)}) async-start(), calls=%async_computation.3 | async-start | bytes 1310720 | tf_op jit(solution)/shard_map/all_gather | solution.py:21
  133.5 59.2 %copy-start.2 = (f32[1024,64]{0,1:T(8,128)}, f32[1024,64]{0,1:T(8,128)S(1)}, u32[]{:S(2)}) copy-start(f32[1024,64]{0,1:T(8,128)S(1)} %broadcast_multiply_fusion.1) | copy-start | bytes 786436
  157.5 84.5 %all-gather.6.cloned.1.call-start = ((), (), s32[]{:S(2)}) async-start(), calls=%async_computation.4 | async-start | bytes 2359296 | tf_op jit(solution)/shard_map/all_gather | solution.py:23
  173.7 71.6 %copy-start.1 = (f32[4096,64]{0,1:T(8,128)S(1)}, f32[4096,64]{0,1:T(8,128)}, u32[]{:S(2)}) copy-start(f32[4096,64]{0,1:T(8,128)} %all-gather.4.cloned.1.call-done) | copy-start | bytes 3145732
  245.3 15.3 %copy-start.3 = (f32[1024,64]{0,1:T(8,128)}, f32[1024,64]{0,1:T(8,128)S(1)}, u32[]{:S(2)}) copy-start(f32[1024,64]{0,1:T(8,128)S(1)} %broadcast_multiply_fusion) | copy-start | bytes 786436
Sparse Core Ops, SparseCore 0:
  30.6 27.4 reduce-scatter.1
  61.5 71.0 all-reduce.1
  157.6 16.0 all-gather.3
  192.9 49.0 all-gather.5
